TPU v7x, 256 devices: a whole 4x4x8 slice. The times are simulated.
256 devices in a mesh: seq: 64 (over z, y, x_lo), tp: 4 (over x_hi, core).
Axes of the slice: x: 4 (x_hi: 2, x_lo: 2; x = x_hi * 2 + x_lo), y: 4, z: 8, core: 2. Of those that a mesh axis runs over, the one named last changes fastest.
Arguments:
- hidden_in: bfloat16 [24576, 3072], P('seq', 'tp'), may hold values from -6 to 6
- norm_gain: bfloat16 [3072], replicated, may hold values from 0.5 to 1.5
- w_query: bfloat16 [3072, 1536], P(None, 'tp')
- w_key: bfloat16 [3072, 512], P(None, 'tp')
- w_value: bfloat16 [3072, 512], P(None, 'tp'), may hold values from -0.109375 to 0.109375
- w_out: bfloat16 [1536, 3072], P('tp'), may hold values from -0.3125 to 0.3125
- short_lengths: int32 [14], replicated, may hold values from 256 to 1024, as said below
- page_slot: int32 [384], replicated, may hold values from 0 to 383, each once
Outputs:
- hidden_out: bfloat16 [24576, 3072], P('seq', 'tp')
- cache_pool: bfloat16 [384, 2, 64, 512], P('seq', None, None, 'tp')
Inputs may be any that keep to these rules, and one draw needn't show every extreme that they name: `short_lengths`: multiples of 64; at least one short prompt has 1024 tokens; together they have 24576 - 16512 tokens. `page_slot`: each slot is named by exactly one page.
All inputs are finite; a program needn't handle non-finite values.
Results may differ from a plain program's by a relative error of at most 0.015.
Values may be sent and summed in bfloat16 or wider, within the bound.
A program may use at most 128 MiB of HBM per device.

v0:
```python
import jax
import jax.numpy as jnp
from jax import lax
from jax.sharding import PartitionSpec as P

QH = 12
KVH = 4
HD = 128
PAGE = 64
rope_base = 500000.0
norm_eps = 1e-05
neg_large = -1e30


def packed_position(row_ids, rows_per_dev, seq_count):
    block_rows = rows_per_dev // 2
    device = row_ids // rows_per_dev
    second = row_ids // block_rows % 2
    block_id = jnp.where(second == 0, device, 2 * seq_count - 1 - device)
    return block_id * block_rows + row_ids % block_rows


def storage_row(positions, rows_per_dev, seq_count):
    block_rows = rows_per_dev // 2
    block_id = positions // block_rows
    device = jnp.where(block_id < seq_count, block_id, 2 * seq_count - 1 - block_id)
    second = jnp.where(block_id < seq_count, 0, 1)
    return device * rows_per_dev + second * block_rows + positions % block_rows


def prompt_start(positions, short_lengths, long_len):
    prompt_ends = long_len + jnp.cumsum(short_lengths)
    bounds = jnp.concatenate(
        [jnp.zeros((1,), jnp.int32), jnp.reshape(long_len, (1,)), prompt_ends[:-1]]
    )
    at_or_before = bounds[None, :] <= positions[:, None]
    return jnp.max(jnp.where(at_or_before, bounds[None, :], 0), axis=1)


def rotate(values, relative, head_size):
    half_size = head_size // 2
    frequency = rope_base ** (-(jnp.arange(half_size, dtype=jnp.float32) * 2.0) / head_size)
    angles = relative.astype(jnp.float32)[:, None] * frequency[None, :]
    cosine = jnp.concatenate([jnp.cos(angles), jnp.cos(angles)], axis=1)[:, None, :]
    sine_part = jnp.concatenate([jnp.sin(angles), jnp.sin(angles)], axis=1)[:, None, :]
    turned = jnp.concatenate([-values[..., half_size:], values[..., :half_size]], axis=-1)
    return values * cosine + turned * sine_part


def project(row_data, norm_gain, w_query, w_key, w_value, relative, head_size):
    wide = row_data.astype(jnp.float32)
    squares = jnp.mean(wide * wide, axis=1, keepdims=True)
    normed = (wide * lax.rsqrt(squares + norm_eps) * norm_gain.astype(jnp.float32)[None, :]).astype(
        jnp.bfloat16
    )
    row_count = row_data.shape[0]
    query_rows = jnp.dot(normed, w_query, preferred_element_type=jnp.float32).reshape(
        row_count, -1, head_size
    )
    key_rows = jnp.dot(normed, w_key, preferred_element_type=jnp.float32).reshape(
        row_count, -1, head_size
    )
    value_rows = jnp.dot(normed, w_value, preferred_element_type=jnp.float32).astype(jnp.bfloat16)
    query_rows = rotate(query_rows, relative, head_size).astype(jnp.bfloat16).reshape(row_count, -1)
    key_rows = rotate(key_rows, relative, head_size).astype(jnp.bfloat16).reshape(row_count, -1)
    return (query_rows, key_rows, value_rows)


def attend_block(carried, query_blk, key_blk, value_blk, allowed_pairs, group_size, head_size):
    running_max, denominator, accumulated = carried
    row_count = query_blk.shape[0]
    key_count = key_blk.shape[0]
    queries = query_blk.reshape(row_count, -1, group_size, head_size)
    keys_local = key_blk.reshape(key_count, -1, head_size)
    values_local = value_blk.reshape(key_count, -1, head_size)
    scores = jnp.einsum(
        "rkgd,skd->rkgs", queries, keys_local, preferred_element_type=jnp.float32
    ) * (1.0 / jnp.sqrt(jnp.float32(head_size)))
    visible = allowed_pairs[:, None, None, :]
    scores = jnp.where(visible, scores, neg_large)
    new_max = jnp.maximum(running_max, jnp.max(scores, axis=-1))
    weights = jnp.where(visible, jnp.exp(scores - new_max[..., None]), 0.0)
    factor = jnp.exp(running_max - new_max)
    denominator = denominator * factor + jnp.sum(weights, axis=-1)
    accumulated = accumulated * factor[..., None] + jnp.einsum(
        "rkgs,skd->rkgd",
        weights.astype(jnp.bfloat16),
        values_local,
        preferred_element_type=jnp.float32,
    )
    return (new_max, denominator, accumulated)


def local(hidden_in, norm_gain, w_query, w_key, w_value, w_out, short_lengths, page_slot):
    seq_count = lax.axis_size("seq")
    seq_index = lax.axis_index("seq")
    rows_per_dev = hidden_in.shape[0]
    block_rows = rows_per_dev // 2
    head_size = HD
    group_size = QH // KVH
    total_rows = rows_per_dev * seq_count
    long_len = total_rows - jnp.sum(short_lengths)
    gathered = lax.all_gather(hidden_in, "tp", axis=1, tiled=True)
    row_ids = seq_index * rows_per_dev + jnp.arange(rows_per_dev, dtype=jnp.int32)
    positions = packed_position(row_ids, rows_per_dev, seq_count)
    prompt_first = prompt_start(positions, short_lengths, long_len)
    query_rows, key_rows, value_rows = project(
        gathered, norm_gain, w_query, w_key, w_value, positions - prompt_first, head_size
    )
    kv_heads = key_rows.shape[1] // head_size
    key_width = key_rows.shape[1]
    pages_dev = rows_per_dev // PAGE
    slot_ids = seq_index * pages_dev + jnp.arange(pages_dev, dtype=jnp.int32)
    page_ids = jnp.arange(page_slot.shape[0], dtype=jnp.int32)
    wanted = jnp.sum(
        jnp.where(page_slot[None, :] == slot_ids[:, None], page_ids[None, :], 0), axis=1
    )
    wanted_pos = wanted[:, None] * PAGE + jnp.arange(PAGE, dtype=jnp.int32)[None, :]
    wanted_rows = storage_row(wanted_pos, rows_per_dev, seq_count)

    def empty_state():
        return (
            jnp.full((block_rows, kv_heads, group_size), neg_large, jnp.float32),
            jnp.zeros((block_rows, kv_heads, group_size), jnp.float32),
            jnp.zeros((block_rows, kv_heads, group_size, head_size), jnp.float32),
        )

    half_states = (empty_state(), empty_state())
    page_pool = jnp.zeros((pages_dev, 2, PAGE, key_width), jnp.bfloat16)
    key_piece = lax.all_gather(key_rows, "seq", axis=0, tiled=True)
    value_piece = lax.all_gather(value_rows, "seq", axis=0, tiled=True)
    row_count = key_piece.shape[0]
    sub_rows = min(row_count, block_rows)
    sub_count = row_count // sub_rows
    new_states = []
    for fold_half_index in range(2):
        query_blk = query_rows[fold_half_index * block_rows : (fold_half_index + 1) * block_rows]
        query_pos = positions[fold_half_index * block_rows : (fold_half_index + 1) * block_rows]
        query_first = prompt_first[
            fold_half_index * block_rows : (fold_half_index + 1) * block_rows
        ]

        def over_keys(step_index, state_now):
            local_first = step_index * sub_rows
            key_blk = lax.dynamic_slice_in_dim(key_piece, local_first, sub_rows, 0)
            value_blk = lax.dynamic_slice_in_dim(value_piece, local_first, sub_rows, 0)
            key_pos = packed_position(
                local_first + jnp.arange(sub_rows, dtype=jnp.int32), rows_per_dev, seq_count
            )
            allowed_pairs = (key_pos[None, :] >= query_first[:, None]) & (
                key_pos[None, :] <= query_pos[:, None]
            )

            def attend_now(state_in):
                return attend_block(
                    state_in, query_blk, key_blk, value_blk, allowed_pairs, group_size, head_size
                )

            def keep_state(state_in):
                return state_in

            return lax.cond(jnp.any(allowed_pairs), attend_now, keep_state, state_now)

        new_states.append(lax.fori_loop(0, sub_count, over_keys, half_states[fold_half_index]))
    inside = (wanted_rows >= 0) & (wanted_rows < row_count)
    picked = jnp.clip(wanted_rows, 0, row_count - 1).reshape(-1)
    taken_keys = jnp.take(key_piece, picked, axis=0).reshape(pages_dev, PAGE, key_width)
    taken_values = jnp.take(value_piece, picked, axis=0).reshape(pages_dev, PAGE, key_width)
    taken = jnp.stack([taken_keys, taken_values], axis=1)
    page_pool = jnp.where(inside[:, None, :, None], taken, page_pool)
    final_states, page_pool = ((new_states[0], new_states[1]), page_pool)
    attended_parts = []
    for half_index in range(2):
        running_max, denominator, accumulated = final_states[half_index]
        attended_parts.append(
            (accumulated / denominator[..., None]).astype(jnp.bfloat16).reshape(block_rows, -1)
        )
    attended = jnp.concatenate(attended_parts, axis=0)
    column_count = hidden_in.shape[1]
    partial_terms = jnp.dot(attended, w_out, preferred_element_type=jnp.float32)
    summed = lax.psum(partial_terms.astype(jnp.bfloat16), "tp").astype(jnp.float32)
    own_share = lax.dynamic_slice_in_dim(
        summed, lax.axis_index("tp") * column_count, column_count, 1
    )
    hidden_out = (hidden_in.astype(jnp.float32) + own_share).astype(jnp.bfloat16)
    return (hidden_out, page_pool)


def solution(mesh):
    placed = (
        P("seq", "tp"),
        P(),
        P(None, "tp"),
        P(None, "tp"),
        P(None, "tp"),
        P("tp", None),
        P(),
        P(),
    )
    return jax.shard_map(
        local,
        mesh=mesh,
        in_specs=placed,
        out_specs=(P("seq", "tp"), P("seq", None, None, "tp")),
        check_vma=False,
    )
```

profile of v0, /device:TPU:1, one launch (start us, length us, event | category | flops | bytes accessed | tf_op | source)
XLA Modules:
  0.0 1440.1 jit_solution(391605902127887108)
XLA Ops:
  8.7 1.3 reduce_sum.49
  10.0 0.8 reduce-window.9
  12.1 32.6 %all-gather.4.cloned.1.call-done = bf16[384,3072]{1,0:T(8,128)(2,1)} async-done(((bf16[384,768]{1,0:T(8,128)(2,1)}), bf16[384,3072]{1,0:T(8,128)(2,1)}) %all-gather.4.cloned.1.call-update) | async-done | bytes 2359312 | tf_op jit(solution)/shard_map/all_gather | solution.py:103
  44.7 2.2 fusion.46
  46.9 2.8 fusion.83
  50.5 3.3 convolution_convert_fusion.1
  54.4 4.7 fusion.81
  59.1 1.4 copy.42
  61.9 254.3 %all-gather.6.cloned.1.call-done = bf16[24576,128]{0,1:T(8,128)(2,1)} async-done(((bf16[384,128]{0,1:T(8,128)(2,1)}), bf16[24576,128]{0,1:T(8,128)(2,1)}) %all-gather.6.cloned.1.call-update) | async-done | bytes 6291472 | tf_op jit(solution)/shard_map/all_gather | solution.py:130
  316.2 8.6 copy.46
  324.8 300.8 %all-gather.8.cloned.1.call-done = bf16[24576,128]{1,0:T(8,128)(2,1)} async-done(((bf16[384,128]{1,0:T(8,128)(2,1)}), bf16[24576,128]{1,0:T(8,128)(2,1)}) %all-gather.8.cloned.1.call-update) | async-done | bytes 6291472 | tf_op jit(solution)/shard_map/all_gather | solution.py:131
  625.6 190.6 %while.40 = (s32[]{:T(128)}, f32[192,1,3]{0,2,1:T(4,128)S(1)}, f32[192,1,3]{0,2,1:T(4,128)S(1)}, f32[192,1,3,128]{3,0,2,1:T(8,128)S(1)}, s32[192]{0:T(256)S(1)},...) while((s32[]{:T(128)}, f32[192,1,3]{0,2,1:T(4,128)S(1)}, ...), condition=%wide.region_10.11_spmd, body=%wide.region_4.10_spmd.sunk | while | flops 57921800 | bytes 2350373 | solution.py:164
  627.1 2.5 conditional.4
  627.1 1.1 fusion.85
  628.2 1.2 fusion.2
  631.1 0.8 compare_and_fusion.6
  816.6 195.5 %while.41 = (s32[]{:T(128)}, f32[192,1,3]{0,2,1:T(4,128)S(1)}, f32[192,1,3]{0,2,1:T(4,128)S(1)}, f32[192,1,3,128]{3,0,2,1:T(8,128)S(1)}, s32[192]{0:T(256)S(1)},...) while((s32[]{:T(128)}, f32[192,1,3]{0,2,1:T(4,128)S(1)}, ...), condition=%wide.region_17.18_spmd, body=%wide.region_11.17_spmd.sunk | while | flops 57921800 | bytes 2350373 | solution.py:164
  819.5 2.5 conditional.5
  819.5 1.1 fusion.86
  820.6 1.2 fusion.25
  824.9 2.5 conditional.5
  824.9 1.1 fusion.86
  826.0 1.2 fusion.25
  830.3 2.5 conditional.5
  830.4 1.1 fusion.86
  831.5 1.2 fusion.25
  1012.5 2.8 convolution_convert_fusion
  1016.0 4.8 gather_fusion
  1020.7 4.8 gather_fusion.1
  1025.6 0.8 maximum_select_fusion
  1026.4 405.1 %all-reduce.2.cloned.1.call-done = bf16[384,3072]{1,0:T(8,128)(2,1)} async-done(((bf16[384,3072]{1,0:T(8,128)(2,1)}), bf16[384,3072]{1,0:T(8,128)(2,1)}) %all-reduce.2.cloned.1.call-update) | async-done | bytes 2359312 | tf_op jit(solution)/shard_map/psum | solution.py:181
  1431.5 2.0 add_convert_fusion
  (836 shorter events, 208.4 us)
Async XLA Ops:
  7.2 1005.3 %copy-start = (bf16[384,3072]{1,0:T(8,128)(2,1)S(1)}, bf16[384,3072]{1,0:T(8,128)(2,1)}, u32[]{:S(2)}) copy-start(bf16[384,3072]{1,0:T(8,128)(2,1)} %param.23) | copy-start | bytes 7077892
  7.2 37.5 %all-gather.4.cloned.1.call-start = ((), (), s32[]{:S(2)}) async-start(), calls=%async_computation | async-start | bytes 2949120 | tf_op jit(solution)/shard_map/all_gather | solution.py:103
  7.9 308.3 %all-gather.6.cloned.1.call-start = ((), (), s32[]{:S(2)}) async-start(), calls=%async_computation.1 | async-start | bytes 6389760 | tf_op jit(solution)/shard_map/all_gather | solution.py:130
  50.5 575.1 %all-gather.8.cloned.1.call-start = ((), (), s32[]{:S(2)}) async-start(), calls=%async_computation.2 | async-start | bytes 6389760 | tf_op jit(solution)/shard_map/all_gather | solution.py:131
  53.9 1377.7 %all-reduce.2.cloned.1.call-start = ((), (), s32[]{:S(2)}) async-start(), calls=%async_computation.3 | async-start | bytes 4718592 | tf_op jit(solution)/shard_map/psum | solution.py:181
  1012.1 3.2 copy-start.2
  1012.5 419.1 %copy-start.1 = (bf16[384,768]{1,0:T(8,128)(2,1)S(1)}, bf16[384,768]{1,0:T(8,128)(2,1)}, u32[]{:S(2)}) copy-start(bf16[384,768]{1,0:T(8,128)(2,1)} %param.18) | copy-start | bytes 1769476
Sparse Core Ops, SparseCore 0:
  9.8 34.8 all-gather.3
  50.6 265.5 all-gather.5
  318.0 307.5 all-gather.7
  1015.4 416.0 all-reduce.1
where the time goes:
time: 1460 us; the launch traced here: 1440 us
  waiting for transfers between devices  993 us (68%)
  other arithmetic  210 us (14%)
  loops' own time  178 us (12%)
  matrix products  22.8 us (2%)
  local copies, waits for them, and re-layouts  20.6 us (1%)
  between operations  14.7 us (1%)
    psum x1, waiting for transfers between devices, local(): lax.psum(partial_terms.astype(jnp.bfloat16), 'tp').astype(jnp.float32)  405 us
    all_gather x1, waiting for transfers between devices, local(): value_piece = lax.all_gather(value_rows, 'seq', axis=0, tiled=True)  301 us
    all_gather x1, waiting for transfers between devices, local(): key_piece = lax.all_gather(key_rows, 'seq', axis=0, tiled=True)  254 us
    and x256, other arithmetic, over_keys(): (key_pos[None, :] >= query_first[:, None]) & (key_pos[None, :] <= query_p...  192 us
    another operation x2, loops' own time, local(): lax.fori_loop(0, sub_count, over_keys, half_states[fold_half_index])  174 us
    all_gather x1, waiting for transfers between devices, local(): gathered = lax.all_gather(hidden_in, 'tp', axis=1, tiled=True)  32.6 us
  transfers between devices with their start and end apart: 4, of which 4 were waited for; matrix products, arithmetic and copies ran while one was open for 2% of the time, Pallas kernels for 0%

commit v1 on v0

--- a/solution.py
+++ b/solution.py
@@ -127,8 +127,11 @@
 
     half_states = (empty_state(), empty_state())
     page_pool = jnp.zeros((pages_dev, 2, PAGE, key_width), jnp.bfloat16)
-    key_piece = lax.all_gather(key_rows, "seq", axis=0, tiled=True)
-    value_piece = lax.all_gather(value_rows, "seq", axis=0, tiled=True)
+    key_piece, value_piece = jnp.split(
+        lax.all_gather(jnp.concatenate([key_rows, value_rows], axis=1), "seq", axis=0, tiled=True),
+        [key_rows.shape[1]],
+        axis=1,
+    )
     row_count = key_piece.shape[0]
     sub_rows = min(row_count, block_rows)
     sub_count = row_count // sub_rows

time: 1460 us -> 1190 us (0.82)
  waiting for transfers between devices: 993 us -> 710 us
  local copies, waits for them, and re-layouts: 20.6 us -> 40.6 us
    all_gather x2 -> x1, waiting for transfers between devices: 555 us -> 273 us  [local(): lax.all_gather(jnp.concatenate([key_rows, value_rows], axis=1), 'seq', ax...]
  transfers between devices with their start and end apart: 4 -> 3, of which waited for: 4 -> 3; matrix products, arithmetic and copies ran while one was open for 2% -> 2% of each run, Pallas kernels for 0% -> 0%
where the time goes in v1:
time: 1190 us; the launch traced here: 1170 us
  waiting for transfers between devices  710 us (60%)
  other arithmetic  211 us (18%)
  loops' own time  178 us (15%)
  local copies, waits for them, and re-layouts  40.6 us (3%)
  matrix products  20.4 us (2%)
  between operations  14.7 us (1%)
    psum x1, waiting for transfers between devices, local(): lax.psum(partial_terms.astype(jnp.bfloat16), 'tp').astype(jnp.float32)  403 us
    all_gather x1, waiting for transfers between devices, local(): lax.all_gather(jnp.concatenate([key_rows, value_rows], axis=1), 'seq', ax...  273 us
    and x256, other arithmetic, over_keys(): (key_pos[None, :] >= query_first[:, None]) & (key_pos[None, :] <= query_p...  192 us
    another operation x2, loops' own time, local(): lax.fori_loop(0, sub_count, over_keys, half_states[fold_half_index])  174 us
    all_gather x1, waiting for transfers between devices, local(): gathered = lax.all_gather(hidden_in, 'tp', axis=1, tiled=True)  32.6 us
  transfers between devices with their start and end apart: 3, of which 3 were waited for; matrix products, arithmetic and copies ran while one was open for 2% of the time, Pallas kernels for 0%

profile of v1, /device:TPU:1, one launch (start us, length us, event | category | flops | bytes accessed | tf_op | source)
XLA Modules:
  0.0 1174.8 jit_solution(6789728171823273963)
XLA Ops:
  8.0 1.3 reduce_sum.49
  9.3 0.8 reduce-window.9
  12.1 32.6 %all-gather.3.cloned.1.call-done = bf16[384,3072]{1,0:T(8,128)(2,1)} async-done(((bf16[384,768]{1,0:T(8,128)(2,1)}), bf16[384,3072]{1,0:T(8,128)(2,1)}) %all-gather.3.cloned.1.call-update) | async-done | bytes 2359312 | tf_op jit(solution)/shard_map/all_gather | solution.py:103
  44.7 2.4 fusion.46
  47.1 2.8 fusion.83
  50.6 1.0 convolution_convert_fusion.1
  52.7 4.7 fusion.80
  57.4 1.4 copy.48
  58.9 1.1 copy.51
  61.3 273.2 %all-gather.5.cloned.1.call-done = bf16[24576,256]{0,1:T(8,128)(2,1)} async-done(((bf16[384,256]{0,1:T(8,128)(2,1)}), bf16[24576,256]{0,1:T(8,128)(2,1)}) %all-gather.5.cloned.1.call-update) | async-done | bytes 12582928 | tf_op jit(solution)/shard_map/all_gather | solution.py:131
  334.5 10.4 fusion.87
  344.9 8.6 copy.53
  353.5 8.6 copy.52
  362.2 195.6 %while.41 = (s32[]{:T(128)}, f32[192,1,3]{0,2,1:T(4,128)S(1)}, f32[192,1,3]{0,2,1:T(4,128)S(1)}, f32[192,1,3,128]{3,0,2,1:T(8,128)S(1)}, s32[192]{0:T(256)S(1)},...) while((s32[]{:T(128)}, f32[192,1,3]{0,2,1:T(4,128)S(1)}, ...), condition=%wide.region_17.18_spmd, body=%wide.region_11.17_spmd.sunk | while | flops 57921800 | bytes 2350373 | solution.py:167
  365.1 2.5 conditional.5
  365.1 1.1 fusion.86
  366.2 1.2 fusion.25
  370.5 2.5 conditional.5
  370.5 1.1 fusion.86
  371.6 1.2 fusion.25
  375.9 2.5 conditional.5
  375.9 1.1 fusion.86
  377.0 1.2 fusion.25
  557.8 190.6 %while.40 = (s32[]{:T(128)}, f32[192,1,3]{0,2,1:T(4,128)S(1)}, f32[192,1,3]{0,2,1:T(4,128)S(1)}, f32[192,1,3,128]{3,0,2,1:T(8,128)S(1)}, s32[192]{0:T(256)S(1)},...) while((s32[]{:T(128)}, f32[192,1,3]{0,2,1:T(4,128)S(1)}, ...), condition=%wide.region_10.11_spmd, body=%wide.region_4.10_spmd.sunk | while | flops 57921800 | bytes 2350373 | solution.py:167
  559.3 2.5 conditional.4
  559.3 1.1 fusion.85
  560.4 1.2 fusion.2
  749.1 2.8 convolution_convert_fusion
  752.6 4.8 gather_fusion.1
  757.4 4.8 gather_fusion
  763.1 403.2 %all-reduce.2.cloned.1.call-done = bf16[384,3072]{1,0:T(8,128)(2,1)} async-done(((bf16[384,3072]{1,0:T(8,128)(2,1)}), bf16[384,3072]{1,0:T(8,128)(2,1)}) %all-reduce.2.cloned.1.call-update) | async-done | bytes 2359312 | tf_op jit(solution)/shard_map/psum | solution.py:184
  1166.2 2.0 add_convert_fusion
  (840 shorter events, 210.5 us)
Async XLA Ops:
  7.2 741.9 %copy-start = (bf16[384,3072]{1,0:T(8,128)(2,1)S(1)}, bf16[384,3072]{1,0:T(8,128)(2,1)}, u32[]{:S(2)}) copy-start(bf16[384,3072]{1,0:T(8,128)(2,1)} %param.23) | copy-start | bytes 7077892
  7.2 37.5 %all-gather.3.cloned.1.call-start = ((), (), s32[]{:S(2)}) async-start(), calls=%async_computation | async-start | bytes 2949120 | tf_op jit(solution)/shard_map/all_gather | solution.py:103
  7.9 326.6 %all-gather.5.cloned.1.call-start = ((), (), s32[]{:S(2)}) async-start(), calls=%async_computation.1 | async-start | bytes 12779520 | tf_op jit(solution)/shard_map/all_gather | solution.py:131
  44.7 5.9 copy-start.1
  44.7 5.9 copy-start.4
  52.4 1113.9 %all-reduce.2.cloned.1.call-start = ((), (), s32[]{:S(2)}) async-start(), calls=%async_computation.2 | async-start | bytes 4718592 | tf_op jit(solution)/shard_map/psum | solution.py:184
  748.6 3.4 copy-start.3
  749.1 417.1 %copy-start.2 = (bf16[384,768]{1,0:T(8,128)(2,1)S(1)}, bf16[384,768]{1,0:T(8,128)(2,1)}, u32[]{:S(2)}) copy-start(bf16[384,768]{1,0:T(8,128)(2,1)} %param.18) | copy-start | bytes 1769476
Sparse Core Ops, SparseCore 0:
  9.8 34.8 all-gather.2
  52.5 282.0 all-gather.4
  752.0 414.1 all-reduce.1
